TPU v7x, 32 devices: a whole 2x2x4 slice. The times are simulated.
32 devices in a mesh: tok: 4 (over y, core), ch: 8 (over z, x).
Axes of the slice: x: 2, y: 2, z: 4, core: 2. Of those that a mesh axis runs over, the one named last changes fastest.
Arguments:
- tokens: bfloat16 [4096, 4096], P('tok', 'ch'), may hold values from -6 to 6
- w_in: bfloat16 [4096, 16384], P('tok', 'ch'), may hold values from -0.09375 to 0.09375
- b_in: float32 [16384], P('ch'), may hold values from -3 to 3
- dw_kernel: float32 [9, 16384], P(None, 'ch'), may hold values from -2 to 2
- dw_bias: float32 [16384], P('ch'), may hold values from -3 to 3
- w_out: bfloat16 [16384, 4096], P('ch', 'tok'), may hold values from -0.0625 to 0.0625
- b_out: float32 [4096], P('ch'), may hold values from -3 to 3
Outputs:
- mixed: bfloat16 [4096, 4096], P('tok', 'ch')
All inputs are finite; a program needn't handle non-finite values.
Results may differ from a plain program's by a relative error of at most 0.0055.
Values may be sent and summed in bfloat16 or wider, within the bound.
No kernel may reach another device: no remote copies, remote signals or barrier semaphores. Data moves between devices by JAX's collectives and lax.ppermute only.
A program may use at most 128 MiB of HBM per device.

v0:
```python
import jax
import jax.numpy as jnp
from jax import lax
from jax.sharding import PartitionSpec as P

IMAGES = 2
GRIDW = 64


def with_halo(array, sides, width):
    for axis, dim in sides:
        size, length = (lax.axis_size(axis), array.shape[dim])
        up = [(i, (i + 1) % size) for i in range(size - 1)]
        down = [(j, i) for i, j in up]
        last = lax.slice_in_dim(array, length - width, length, axis=dim)
        initial = lax.slice_in_dim(array, 0, width, axis=dim)
        before = lax.ppermute(last, axis, up)
        after = lax.ppermute(initial, axis, down)
        array = jnp.concatenate([before, array, after], axis=dim)
    return array


def fetch_rims(grid):
    return with_halo(grid, (("tok", 0),), 1)


def conv_taps(padded, taps, bias, height, width):
    conv = bias + jnp.zeros(
        (height,) + padded.shape[1:2] + (width,) + padded.shape[3:], jnp.float32
    )
    for row_off in range(3):
        for col_off in range(3):
            conv = (
                conv
                + taps[3 * row_off + col_off]
                * padded[row_off : row_off + height, :, col_off : col_off + width, :]
            )
    return conv


def pad_columns(grid):
    return jnp.pad(grid, ((0, 0), (0, 0), (1, 1), (0, 0)))


def local(tokens, w_in, b_in, dw_kernel, dw_bias, w_out, b_out):
    rows = tokens.shape[0]
    hidden = w_in.shape[1]
    w_whole = lax.all_gather(w_in, "tok", axis=0, tiled=True)
    summed = jnp.dot(
        lax.all_gather(tokens, "ch", axis=1, tiled=True),
        w_whole,
        preferred_element_type=jnp.float32,
    )
    pre = (summed + b_in).astype(jnp.bfloat16)
    height = rows // (IMAGES * GRIDW)
    grid = pre.reshape(height, IMAGES, GRIDW, hidden)
    padded = pad_columns(fetch_rims(grid).astype(jnp.float32))
    conv = conv_taps(padded, dw_kernel, dw_bias, height, GRIDW)
    act = jax.nn.gelu(conv, approximate=False).astype(jnp.bfloat16).reshape(rows, hidden)
    w_cols = lax.all_gather(w_out, "tok", axis=1, tiled=True)
    flipped = lax.psum_scatter(
        lax.dot_general(w_cols, act, (((0,), (1,)), ((), ())), preferred_element_type=jnp.float32),
        "ch",
        scatter_dimension=0,
        tiled=True,
    )
    return (flipped.T + b_out).astype(jnp.bfloat16)


def solution(mesh):
    in_specs = (
        P("tok", "ch"),
        P("tok", "ch"),
        P("ch"),
        P(None, "ch"),
        P("ch"),
        P("ch", "tok"),
        P("ch"),
    )
    out_specs = P("tok", "ch")
    return jax.shard_map(local, mesh=mesh, in_specs=in_specs, out_specs=out_specs, check_vma=False)
```

profile of v0, /device:TPU:0, one launch (start us, length us, event | category | flops | bytes accessed | tf_op | source)
XLA Modules:
  0.0 669.0 jit_solution(11230460719229125539)
XLA Ops:
  6.5 0.0 copy-start.3
  6.5 0.0 all-gather.4.cloned.1.call-start
  6.5 0.7 all-gather.4.cloned.1.call-update
  7.3 0.0 all-gather.6.cloned.1.call-start
  7.3 0.7 all-gather.6.cloned.1.call-update
  8.0 0.0 all-gather.8.cloned.1.call-start
  8.1 0.7 all-gather.8.cloned.1.call-update
  8.7 0.0 copy-start
  8.8 0.0 reduce-scatter.2.cloned.1.call-start
  8.8 128.3 %all-gather.4.cloned.1.call-done = bf16[1024,4096]{1,0:T(8,128)(2,1)} async-done(((bf16[1024,512]{1,0:T(8,128)(2,1)}), bf16[1024,4096]{1,0:T(8,128)(2,1)}) %all-gather.4.cloned.1.call-update) | async-done | bytes 8388624 | tf_op jit(solution)/shard_map/all_gather | solution.py:50
  137.1 105.7 %all-gather.6.cloned.1.call-done = bf16[4096,2048]{1,0:T(8,128)(2,1)} async-done(((bf16[1024,2048]{1,0:T(8,128)(2,1)}), bf16[4096,2048]{1,0:T(8,128)(2,1)}) %all-gather.6.cloned.1.call-update) | async-done | bytes 16777232 | tf_op jit(solution)/shard_map/all_gather | solution.py:48
  242.7 0.0 copy-done.3
  242.7 22.7 %add_convert_fusion = bf16[1024,2048]{1,0:T(8,128)(2,1)S(1)} fusion(bf16[1024,4096]{1,0:T(8,128)(2,1)} %all-gather.4.cloned.1.call-done, bf16[4096,2048]{1,0:T(8,128)(2,1)} %all-gather.6.cloned.1.call-done, f32[2048]{0:T(1024)S(1)} %copy-done.3), kind=kOutput, calls=%fused_computation.42 | convolution fusion | flops 17184063488 | bytes 29368320 | tf_op jit(solution)/shard_map/dot_general | solution.py:49
  265.4 0.1 fusion.26
  265.6 0.0 copy-start.1
  265.6 1.3 collective-permute-start.1
  266.9 3.1 collective-permute-start
  269.9 0.0 copy-done
  269.9 0.1 fusion.27
  270.0 0.0 collective-permute-done.1
  270.0 1.9 collective-permute-done
  271.9 0.8 maximum_convert_fusion
  272.7 0.0 copy-done.1
  272.7 27.4 %fusion.17 = bf16[8,2,64,2048]{3,2,1,0:T(8,128)(2,1)} fusion(f32[10,2,64,2048]{3,2,1,0:T(8,128)S(1)} %maximum_convert_fusion, f32[2048]{0:T(1024)S(1)} %bitcast.32, f32[2048]{0:T(1024)S(1)} %bitcast.33, f32[2048]{0:T(1024)S(1)} %bitcast.26, f32[2048]{0:T(1024)S(1)} %bitcast.27, f32[2048]{0:T(1024)S(1)} %bitcast.28, f32[2048]{0:T(1024)S(1)} %bitcast.29, ...), kind=kLoop, calls=%fused_computation.25 | loop fusion | flops 174063616 | bytes 39927808 | tf_op jit(solution)/shard_map/convert_element_type | solution.py:59
  300.2 55.7 %all-gather.8.cloned.1.call-done = bf16[2048,4096]{1,0:T(8,128)(2,1)} async-done(((bf16[2048,1024]{1,0:T(8,128)(2,1)}), bf16[2048,4096]{1,0:T(8,128)(2,1)}) %all-gather.8.cloned.1.call-update) | async-done | bytes 16777232 | tf_op jit(solution)/shard_map/all_gather | solution.py:60
  355.9 23.4 %convolution_bitcast_fusion = f32[4096,1024]{0,1:T(8,128)} fusion(bf16[1024,2048]{1,0:T(8,128)(2,1)} %bitcast.22, bf16[2048,4096]{1,0:T(8,128)(2,1)} %all-gather.8.cloned.1.call-done), kind=kOutput, calls=%fused_computation.7 | convolution fusion | flops 17179869184 | bytes 37748736 | tf_op jit(solution)/shard_map/dot_general | solution.py:62
  379.3 0.0 copy-start.2
  379.3 0.0 reduce-scatter.2.cloned.1.call-update
  379.3 280.3 %reduce-scatter.2.cloned.1.call-done = f32[512,1024]{0,1:T(8,128)} async-done(((f32[4096,1024]{0,1:T(8,128)}), f32[512,1024]{0,1:T(8,128)}) %reduce-scatter.2.cloned.1.call-update) | async-done | bytes 2097168 | tf_op jit(solution)/shard_map/reduce_scatter | solution.py:61
  659.6 0.0 copy-done.2
  659.6 2.8 fusion.25
Async XLA Ops:
  6.5 236.2 %copy-start.3 = (f32[2048]{0:T(1024)S(1)}, f32[2048]{0:T(1024)}, u32[]{:S(2)}) copy-start(f32[2048]{0:T(1024)} %param.9) | copy-start | bytes 24580
  6.5 130.5 %all-gather.4.cloned.1.call-start = ((), (), s32[]{:S(2)}) async-start(), calls=%async_computation.1 | async-start | bytes 9437184 | tf_op jit(solution)/shard_map/all_gather | solution.py:50
  7.3 235.5 %all-gather.6.cloned.1.call-start = ((), (), s32[]{:S(2)}) async-start(), calls=%async_computation.2 | async-start | bytes 20971520 | tf_op jit(solution)/shard_map/all_gather | solution.py:48
  8.0 347.9 %all-gather.8.cloned.1.call-start = ((), (), s32[]{:S(2)}) async-start(), calls=%async_computation.3 | async-start | bytes 20971520 | tf_op jit(solution)/shard_map/all_gather | solution.py:60
  8.7 261.2 %copy-start = (f32[9,2048]{1,0:T(8,128)S(1)}, f32[9,2048]{1,0:T(8,128)}, u32[]{:S(2)}) copy-start(f32[9,2048]{1,0:T(8,128)} %param.10) | copy-start | bytes 221188
  8.8 650.8 %reduce-scatter.2.cloned.1.call-start = ((), (), s32[]{:S(2)}) async-start(), calls=%async_computation.4 | async-start | bytes 18874368 | tf_op jit(solution)/shard_map/reduce_scatter | solution.py:61
  265.6 7.2 %copy-start.1 = (f32[2048]{0:T(1024)S(1)}, f32[2048]{0:T(1024)}, u32[]{:S(2)}) copy-start(f32[2048]{0:T(1024)} %param.11) | copy-start | bytes 24580
  265.6 4.4 collective-permute-start.1
  266.9 5.0 collective-permute-start
  379.3 280.3 %copy-start.2 = (f32[512]{0:T(512)S(1)}, f32[512]{0:T(512)}, u32[]{:S(2)}) copy-start(f32[512]{0:T(512)} %param.13) | copy-start | bytes 6148
Sparse Core Ops, SparseCore 0:
  9.4 127.6 all-gather.3
  138.6 104.0 all-gather.5
  244.3 111.5 all-gather.7
  379.4 280.1 reduce-scatter.1
where the time goes:
time: 669 us
  waiting for transfers between devices  574 us (86%)
  matrix products  46.1 us (7%)
  other arithmetic  31.1 us (5%)
  between operations  13.2 us (2%)
    reduce_scatter x1, waiting for transfers between devices, local(): lax.psum_scatter(lax.dot_general(w_cols, act, (((0,), (1,)), ((), ())), p...  280 us
    all_gather x1, waiting for transfers between devices, local(): lax.all_gather(tokens, 'ch', axis=1, tiled=True)  128 us
    all_gather x1, waiting for transfers between devices, local(): w_whole = lax.all_gather(w_in, 'tok', axis=0, tiled=True)  106 us
    all_gather x1, waiting for transfers between devices, local(): w_cols = lax.all_gather(w_out, 'tok', axis=1, tiled=True)  55.7 us
    convert_element_type x1, other arithmetic, local(): jax.nn.gelu(conv, approximate=False).astype(jnp.bfloat16)  27.4 us
    dot_general x1, matrix products, local(): lax.dot_general(w_cols, act, (((0,), (1,)), ((), ())), preferred_element_...  23.4 us
    dot_general x1, matrix products, local(): jnp.dot(lax.all_gather(tokens, 'ch', axis=1, tiled=True), w_whole, prefer...  22.7 us
  transfers between devices with their start and end apart: 6, of which 5 were waited for; matrix products, arithmetic and copies ran while one was open for 8% of the time, Pallas kernels for 0%

commit v1 on v0

--- a/solution.py
+++ b/solution.py
@@ -2,6 +2,7 @@
 import jax.numpy as jnp
 from jax import lax
 from jax.sharding import PartitionSpec as P
+from jax.lax import axis_index, axis_size, ppermute
 
 IMAGES = 2
 GRIDW = 64
@@ -57,7 +58,15 @@
     padded = pad_columns(fetch_rims(grid).astype(jnp.float32))
     conv = conv_taps(padded, dw_kernel, dw_bias, height, GRIDW)
     act = jax.nn.gelu(conv, approximate=False).astype(jnp.bfloat16).reshape(rows, hidden)
-    w_cols = lax.all_gather(w_out, "tok", axis=1, tiled=True)
+    finding, reply, back = (axis_size("tok"), axis_index("tok"), w_out.shape[1])
+    column = tuple(((dev_j, (dev_j + 1) % finding) for dev_j in range(finding)))
+    w_cols = jnp.zeros((*w_out.shape[:1], finding * back, *w_out.shape[1 + 1 :]), w_out.dtype)
+    val2 = w_out
+    for u in range(finding):
+        everything = (reply - u) % finding
+        w_cols = lax.dynamic_update_slice_in_dim(w_cols, val2, everything * back, axis=1)
+        if u < finding - 1:
+            val2 = ppermute(val2, axis_name="tok", perm=column)
     flipped = lax.psum_scatter(
         lax.dot_general(w_cols, act, (((0,), (1,)), ((), ())), preferred_element_type=jnp.float32),
         "ch",

time: 669 us -> 626 us (0.936)
  waiting for transfers between devices: 574 us -> 506 us
  local copies, waits for them, and re-layouts: 0.17 us -> 24.7 us
    all_gather x1, waiting for transfers between devices: 128 us -> 31.8 us  [local(): lax.all_gather(tokens, 'ch', axis=1, tiled=True)]
    ppermute x0 -> x3, waiting for transfers between devices: none -> 82.7 us  [local(): val2 = ppermute(val2, axis_name='tok', perm=column)]
    all_gather x1 -> x0, waiting for transfers between devices: 55.7 us -> none  [local(): w_cols = lax.all_gather(w_out, 'tok', axis=1, tiled=True)]
    dynamic_update_slice x0 -> x4, local copies, waits for them, and re-layouts: none -> 16.5 us  [local(): lax.dynamic_update_slice_in_dim(w_cols, val2, everything * back, axis=1)]
    broadcast_in_dim x0 -> x1, local copies, waits for them, and re-layouts: none -> 6.73 us  [local(): jnp.zeros((*w_out.shape[:1], finding * back, *w_out.shape[1 + 1:]), w_out...]
  transfers between devices with their start and end apart: 6 -> 8, of which waited for: 5 -> 5; matrix products, arithmetic and copies ran while one was open for 8% -> 7% of each run, Pallas kernels for 0% -> 0%
where the time goes in v1:
time: 626 us
  waiting for transfers between devices  506 us (81%)
  matrix products  46.3 us (7%)
  other arithmetic  30.1 us (5%)
  local copies, waits for them, and re-layouts  24.7 us (4%)
  between operations  13.2 us (2%)
    reduce_scatter x1, waiting for transfers between devices, local(): lax.psum_scatter(lax.dot_general(w_cols, act, (((0,), (1,)), ((), ())), p...  282 us
    all_gather x1, waiting for transfers between devices, local(): w_whole = lax.all_gather(w_in, 'tok', axis=0, tiled=True)  108 us
    ppermute x3, waiting for transfers between devices, local(): val2 = ppermute(val2, axis_name='tok', perm=column)  82.7 us
    all_gather x1, waiting for transfers between devices, local(): lax.all_gather(tokens, 'ch', axis=1, tiled=True)  31.8 us
    convert_element_type x1, other arithmetic, local(): jax.nn.gelu(conv, approximate=False).astype(jnp.bfloat16)  27.5 us
    dot_general x1, matrix products, local(): lax.dot_general(w_cols, act, (((0,), (1,)), ((), ())), preferred_element_...  23.6 us
    dot_general x1, matrix products, local(): jnp.dot(lax.all_gather(tokens, 'ch', axis=1, tiled=True), w_whole, prefer...  22.7 us
    dynamic_update_slice x4, local copies, waits for them, and re-layouts, local(): lax.dynamic_update_slice_in_dim(w_cols, val2, everything * back, axis=1)  16.5 us
  transfers between devices with their start and end apart: 8, of which 5 were waited for; matrix products, arithmetic and copies ran while one was open for 7% of the time, Pallas kernels for 0%

profile of v1, /device:TPU:0, one launch (start us, length us, event | category | flops | bytes accessed | tf_op | source)
XLA Modules:
  0.0 625.8 jit_solution(17801438593898503543)
XLA Ops:
  6.5 0.0 all-gather.3.cloned.1.call-start
  6.5 0.7 all-gather.3.cloned.1.call-update
  7.3 0.0 all-gather.5.cloned.1.call-start
  7.3 0.7 all-gather.5.cloned.1.call-update
  8.0 0.0 reduce-scatter.2.cloned.1.call-start
  8.1 0.5 collective-permute-start
  8.6 48.4 %collective-permute-done = bf16[2048,1024]{1,0:T(8,128)(2,1)} collective-permute-done((bf16[2048,1024]{1,0:T(8,128)(2,1)}, bf16[2048,1024]{1,0:T(8,128)(2,1)}, u32[]{:S(2)}, u32[]{:S(2)}) %collective-permute-start) | collective-permute-done | bytes 4194336 | tf_op jit(solution)/shard_map/ppermute | solution.py:69
  57.0 0.0 collective-permute-start.1
  57.0 0.0 copy-start
  57.1 6.7 %broadcast_in_dim.2 = bf16[2048,4096]{1,0:T(8,128)(2,1)} broadcast(bf16[]{:T(256)} %constant.40.clone.1), dimensions={} | broadcast | bytes 16777218 | tf_op jit(solution)/shard_map/broadcast_in_dim | solution.py:63
  63.8 0.0 copy-done
  63.8 0.0 copy-start.1
  63.8 0.0 copy-start.4
  63.8 2.4 constant_dynamic-update-slice_fusion.3
  66.2 0.0 copy-done.1
  66.2 4.8 constant_dynamic-update-slice_fusion.2
  71.0 34.3 %collective-permute-done.1 = bf16[2048,1024]{1,0:T(8,128)(2,1)} collective-permute-done((bf16[2048,1024]{1,0:T(8,128)(2,1)}, bf16[2048,1024]{1,0:T(8,128)(2,1)}, u32[]{:S(2)}, u32[]{:S(2)}) %collective-permute-start.1) | collective-permute-done | bytes 4194336 | tf_op jit(solution)/shard_map/ppermute | solution.py:69
  105.3 0.0 collective-permute-start.2
  105.3 31.8 %all-gather.3.cloned.1.call-done = bf16[1024,4096]{1,0:T(8,128)(2,1)} async-done(((bf16[1024,512]{1,0:T(8,128)(2,1)}), bf16[1024,4096]{1,0:T(8,128)(2,1)}) %all-gather.3.cloned.1.call-update) | async-done | bytes 8388624 | tf_op jit(solution)/shard_map/all_gather | solution.py:51
  137.1 108.4 %all-gather.5.cloned.1.call-done = bf16[4096,2048]{1,0:T(8,128)(2,1)} async-done(((bf16[1024,2048]{1,0:T(8,128)(2,1)}), bf16[4096,2048]{1,0:T(8,128)(2,1)}) %all-gather.5.cloned.1.call-update) | async-done | bytes 16777232 | tf_op jit(solution)/shard_map/all_gather | solution.py:49
  245.5 0.0 copy-done.4
  245.5 22.7 %add_convert_fusion = bf16[1024,2048]{1,0:T(8,128)(2,1)S(1)} fusion(bf16[1024,4096]{1,0:T(8,128)(2,1)} %all-gather.3.cloned.1.call-done, bf16[4096,2048]{1,0:T(8,128)(2,1)} %all-gather.5.cloned.1.call-done, f32[2048]{0:T(1024)S(1)} %copy-done.4), kind=kOutput, calls=%fused_computation.41 | convolution fusion | flops 17184063488 | bytes 29368320 | tf_op jit(solution)/shard_map/dot_general | solution.py:50
  268.2 0.1 fusion.26
  268.3 1.3 collective-permute-start.4
  269.6 3.2 collective-permute-start.3
  272.8 4.7 constant_dynamic-update-slice_fusion.1
  277.5 0.0 collective-permute-done.2
  277.5 4.7 constant_dynamic-update-slice_fusion
  282.2 0.0 copy-start.2
  282.2 0.0 collective-permute-done.4
  282.2 0.0 collective-permute-done.3
  282.2 0.8 maximum_convert_fusion
  283.0 0.0 copy-done.2
  283.0 27.5 %fusion.17 = bf16[8,2,64,2048]{3,2,1,0:T(8,128)(2,1)} fusion(f32[10,2,64,2048]{3,2,1,0:T(8,128)S(1)} %maximum_convert_fusion, f32[2048]{0:T(1024)S(1)} %bitcast.30, f32[2048]{0:T(1024)S(1)} %bitcast.31, f32[2048]{0:T(1024)S(1)} %bitcast.24, f32[2048]{0:T(1024)S(1)} %bitcast.25, f32[2048]{0:T(1024)S(1)} %bitcast.26, f32[2048]{0:T(1024)S(1)} %bitcast.27, ...), kind=kLoop, calls=%fused_computation.24 | loop fusion | flops 174063616 | bytes 39927808 | tf_op jit(solution)/shard_map/convert_element_type | solution.py:60
  310.5 23.6 %fusion.28 = f32[4096,1024]{1,0:T(8,128)} fusion(bf16[2048,4096]{1,0:T(8,128)(2,1)} %constant_dynamic-update-slice_fusion, bf16[1024,2048]{1,0:T(8,128)(2,1)} %bitcast.20), kind=kOutput, calls=%fused_computation.53 | convolution fusion | flops 17179869184 | bytes 37748736 | tf_op jit(solution)/shard_map/dot_general | solution.py:71
  334.1 0.0 copy-start.3
  334.1 0.0 reduce-scatter.2.cloned.1.call-update
  334.1 282.1 %reduce-scatter.2.cloned.1.call-done = f32[512,1024]{1,0:T(8,128)} async-done(((f32[4096,1024]{1,0:T(8,128)}), f32[512,1024]{1,0:T(8,128)}) %reduce-scatter.2.cloned.1.call-update) | async-done | bytes 2097168 | tf_op jit(solution)/shard_map/reduce_scatter | solution.py:70
  616.2 0.0 copy-done.3
  616.2 1.8 fusion.25
  618.0 1.3 copy.8
  (1 shorter events, 0.0 us)
Async XLA Ops:
  6.5 130.5 %all-gather.3.cloned.1.call-start = ((), (), s32[]{:S(2)}) async-start(), calls=%async_computation.1 | async-start | bytes 9437184 | tf_op jit(solution)/shard_map/all_gather | solution.py:51
  7.3 238.2 %all-gather.5.cloned.1.call-start = ((), (), s32[]{:S(2)}) async-start(), calls=%async_computation.2 | async-start | bytes 20971520 | tf_op jit(solution)/shard_map/all_gather | solution.py:49
  8.0 608.2 %reduce-scatter.2.cloned.1.call-start = ((), (), s32[]{:S(2)}) async-start(), calls=%async_computation.3 | async-start | bytes 18874368 | tf_op jit(solution)/shard_map/reduce_scatter | solution.py:70
  8.1 49.0 %collective-permute-start = (bf16[2048,1024]{1,0:T(8,128)(2,1)}, bf16[2048,1024]{1,0:T(8,128)(2,1)}, u32[]{:S(2)}, u32[]{:S(2)}) collective-permute-start(bf16[2048,1024]{1,0:T(8,128)(2,1)} %param.12), channel_id=1, source_target_pairs={{0,8},{8,16},{16,24},{24,0},{1,9},{9,17},{17,25},{25,1},{2,10},{10... | collective-permute-start | bytes 12582920 | tf_op jit(solution)/shard_map/ppermute | solution.py:69
  57.0 48.2 %collective-permute-start.1 = (bf16[2048,1024]{1,0:T(8,128)(2,1)}, bf16[2048,1024]{1,0:T(8,128)(2,1)}, u32[]{:S(2)}, u32[]{:S(2)}) collective-permute-start(bf16[2048,1024]{1,0:T(8,128)(2,1)} %collective-permute-done), channel_id=1, source_target_pairs={{0,8},{8,16},{16,24},{24,0},{1,9},{9,17},{17,25},{25,1},{2,10},{10... | collective-permute-start | bytes 12582920 | tf_op jit(solution)/shard_map/ppermute | solution.py:69
  57.0 6.7 %copy-start = (bf16[2048,1024]{1,0:T(8,128)(2,1)S(1)}, bf16[2048,1024]{1,0:T(8,128)(2,1)}, u32[]{:S(2)}) copy-start(bf16[2048,1024]{1,0:T(8,128)(2,1)} %param.12) | copy-start | bytes 12582916
  63.8 2.4 copy-start.1
  63.8 181.7 %copy-start.4 = (f32[2048]{0:T(1024)S(1)}, f32[2048]{0:T(1024)}, u32[]{:S(2)}) copy-start(f32[2048]{0:T(1024)} %param.9) | copy-start | bytes 24580
  105.3 172.2 %collective-permute-start.2 = (bf16[2048,1024]{1,0:T(8,128)(2,1)}, bf16[2048,1024]{1,0:T(8,128)(2,1)}, u32[]{:S(2)}, u32[]{:S(2)}) collective-permute-start(bf16[2048,1024]{1,0:T(8,128)(2,1)} %collective-permute-done.1), channel_id=1, source_target_pairs={{0,8},{8,16},{16,24},{24,0},{1,9},{9,17},{17,25},{25,1},{2,10},{10... | collective-permute-start | bytes 12582920 | tf_op jit(solution)/shard_map/ppermute | solution.py:69
  268.3 13.9 %collective-permute-start.4 = (bf16[1,2,64,2048]{3,2,1,0:T(8,128)(2,1)S(1)}, bf16[1,2,64,2048]{3,2,1,0:T(8,128)(2,1)S(1)}, u32[]{:S(2)}, u32[]{:S(2)}) collective-permute-start(bf16[1,2,64,2048]{3,2,1,0:T(8,128)(2,1)S(1)} %bitcast.22), channel_id=1, source_target_pairs={{8,0},{16,8},{24,16},{9,1},{17,9},{25,17},{10,2},{18,10},{26,18},{... | collective-permute-start | bytes 1572872 | tf_op jit(solution)/shard_map/ppermute | solution.py:19
  269.6 12.6 %collective-permute-start.3 = (bf16[1,2,64,2048]{3,2,1,0:T(8,128)(2,1)S(1)}, bf16[1,2,64,2048]{3,2,1,0:T(8,128)(2,1)S(1)}, u32[]{:S(2)}, u32[]{:S(2)}) collective-permute-start(bf16[1,2,64,2048]{3,2,1,0:T(8,128)(2,1)S(1)} %bitcast.21), channel_id=1, source_target_pairs={{0,8},{8,16},{16,24},{1,9},{9,17},{17,25},{2,10},{10,18},{18,26},{... | collective-permute-start | bytes 1572872 | tf_op jit(solution)/shard_map/ppermute | solution.py:18
  282.2 0.9 copy-start.2
  334.1 282.1 %copy-start.3 = (f32[512]{0:T(512)S(1)}, f32[512]{0:T(512)}, u32[]{:S(2)}) copy-start(f32[512]{0:T(512)} %param.13) | copy-start | bytes 6148
Sparse Core Ops, SparseCore 0:
  9.4 127.6 all-gather.2
  138.6 106.8 all-gather.4
  334.3 281.9 reduce-scatter.1
